TPU v7x, 32 devices: a whole 2x2x4 slice. The times are simulated.
32 devices in a mesh: rep: 4 (over y, x), seq: 8 (over z, core).
Axes of the slice: x: 2, y: 2, z: 4, core: 2. Of those that a mesh axis runs over, the one named last changes fastest.
Arguments:
- inputs: bfloat16 [4, 2048, 1536], P('rep', 'seq'), may hold values from -13 to 13
- segment_ids: int32 [4, 2048], P('rep'), may hold values from 0 to 7, as said below
- valid_mask: int32 [4, 2048], P('rep'), may hold values from 0 to 1, as said below
- input_weight: bfloat16 [1536, 4608], P('seq'), may hold values from -0.15625 to 0.15625
- output_weight: bfloat16 [1536, 1536], P('seq'), may hold values from -0.15625 to 0.15625
- conv_kernel: float32 [16, 6, 11], replicated, may hold values from -1.2 to 1.2
- head_mix: float32 [8, 2, 2], replicated, may hold values from 0.2 to 1
- first_gain: float32 [1536], replicated, may hold values from 0.5 to 1.5
- second_gain: float32 [1536], replicated, may hold values from 0.5 to 1.5
- group_gain: float32 [1536], replicated, may hold values from 0.5 to 1.5
- gate_weight: bfloat16 [1536, 4096], P(None, 'seq'), may hold values from -0.15625 to 0.15625
- up_weight: bfloat16 [1536, 4096], P(None, 'seq'), may hold values from -0.15625 to 0.15625
- down_weight: bfloat16 [4096, 1536], P('seq'), may hold values from -0.09375 to 0.09375
- cotangent: bfloat16 [4, 2048, 1536], P('rep', 'seq'), may hold values from -17 to 17
Outputs:
- output: bfloat16 [4, 2048, 1536], P('rep', 'seq')
- grad_inputs: bfloat16 [4, 2048, 1536], P('rep', 'seq')
- grad_input_weight: float32 [1536, 4608], P('seq')
- grad_output_weight: float32 [1536, 1536], P('seq')
- grad_kernel: float32 [16, 6, 11], replicated
- grad_mix: float32 [8, 2, 2], replicated
- grad_first_gain: float32 [1536], replicated
- grad_second_gain: float32 [1536], replicated
- grad_group_gain: float32 [1536], replicated
- grad_gate: float32 [1536, 4096], P(None, 'seq')
- grad_up: float32 [1536, 4096], P(None, 'seq')
- grad_down: float32 [4096, 1536], P('seq')
Inputs may be any that keep to these rules, and one draw needn't show every extreme that they name: `segment_ids`: segment ids never fall along a sequence and start at 0. The positions k * 1024 to (k + 1) * 1024 - 1 form frame k; every document lies inside one frame, a frame holds one to four documents, the first frame of the first sequence is a single document of exactly 1024 positions, and every frame of the last sequence holds four documents. `valid_mask`: in each frame the positions with 0 form its tail, at most 256 of them; the first frame of the first sequence has none.
All inputs are finite; a program needn't handle non-finite values.
Results may differ from a plain program's by a relative error of at most 0.02.
Values may be sent and summed in bfloat16 or wider, within the bound.
A program may use at most 384 MiB of HBM per device.

v0:
```python
import jax
import jax.numpy as jnp
from jax import lax
from jax.sharding import PartitionSpec as P

REACH = 4
EPS = 1e-06
HIGHEST = lax.Precision.HIGHEST


def from_behind(x, axis, by):
    count = lax.axis_size(axis)
    pairs = [(i, i + by) for i in range(count) if 0 <= i + by < count]
    return lax.ppermute(x, axis, pairs)


def convolve(logits, kernel, rows, columns):
    rim_rows = kernel.shape[1] - 1
    key_span = kernel.shape[2] - 1
    result = jnp.zeros((logits.shape[0], rows, columns), jnp.float32)
    for row_tap in range(kernel.shape[1]):
        for col_tap in range(kernel.shape[2]):
            weight = kernel[:, row_tap, col_tap][:, None, None]
            result = (
                result
                + weight
                * logits[
                    :,
                    rim_rows - row_tap : rim_rows - row_tap + rows,
                    key_span - col_tap : key_span - col_tap + columns,
                ]
            )
    return result


def convolve_back(grads, kernel):
    rim_rows = kernel.shape[1] - 1
    key_span = kernel.shape[2] - 1
    rows = grads.shape[1] + rim_rows
    columns = grads.shape[2] + key_span
    padded = jnp.pad(grads, ((0, 0), (rim_rows, rim_rows), (key_span, key_span)))
    result = jnp.zeros((grads.shape[0], rows, columns), jnp.float32)
    for row_tap in range(kernel.shape[1]):
        for col_tap in range(kernel.shape[2]):
            weight = kernel[:, row_tap, col_tap][:, None, None]
            result = (
                result + weight * padded[:, row_tap : row_tap + rows, col_tap : col_tap + columns]
            )
    return result


def kernel_grads(grads, logits, taps_rows, taps_cols):
    rim_rows = taps_rows - 1
    key_span = taps_cols - 1
    rows = grads.shape[1]
    columns = grads.shape[2]
    entries = []
    for row_tap in range(taps_rows):
        line_sums = []
        for col_tap in range(taps_cols):
            window_part = logits[
                :,
                rim_rows - row_tap : rim_rows - row_tap + rows,
                key_span - col_tap : key_span - col_tap + columns,
            ]
            line_sums.append(jnp.sum(grads * window_part, axis=(1, 2)))
        entries.append(jnp.stack(line_sums, axis=-1))
    return jnp.stack(entries, axis=1)


def attend_group(operands, mask_ext, mask_own, row_valid, score_scale):
    query_g, key_g, value_g, kernel_g, mixing_g = operands
    rows = mask_own.shape[0]
    columns = mask_own.shape[1]
    raw = jnp.einsum("qhd,khd->hqk", query_g, key_g, preferred_element_type=jnp.float32)
    logits = raw * score_scale * mask_ext
    conv = convolve(logits, kernel_g, rows, columns)
    allowed = mask_own > 0
    peak = jnp.max(jnp.where(allowed, conv, -1e30), axis=-1, keepdims=True)
    peak = jnp.where(row_valid > 0, peak, 0.0)
    expo = jnp.where(allowed, jnp.exp(conv - peak), 0.0)
    denom = jnp.sum(expo, axis=-1, keepdims=True) + 1.0 - row_valid
    prob = expo / denom
    mixed = (
        mixing_g[:, 0][:, None, None] * prob[0][None]
        + mixing_g[:, 1][:, None, None] * prob[1][None]
    )
    mixed_low = mixed.astype(jnp.bfloat16)
    result = jnp.einsum("hqk,khd->qhd", mixed_low, value_g, preferred_element_type=jnp.float32)
    return (result, peak + jnp.log(denom))


def attend_group_back(operands, mask_ext, mask_own, score_scale):
    query_g, key_g, value_g, kernel_g, mixing_g, dresult_g, lse_g = operands
    rows = mask_own.shape[0]
    columns = mask_own.shape[1]
    raw = jnp.einsum("qhd,khd->hqk", query_g, key_g, preferred_element_type=jnp.float32)
    logits = raw * score_scale * mask_ext
    conv = convolve(logits, kernel_g, rows, columns)
    allowed = mask_own > 0
    prob = jnp.where(allowed, jnp.exp(conv - lse_g), 0.0)
    mixed = (
        mixing_g[:, 0][:, None, None] * prob[0][None]
        + mixing_g[:, 1][:, None, None] * prob[1][None]
    )
    mixed_low = mixed.astype(jnp.bfloat16)
    dmixed = jnp.einsum("qhd,khd->hqk", dresult_g, value_g, preferred_element_type=jnp.float32)
    dvalue = jnp.einsum("hqk,qhd->khd", mixed_low, dresult_g, preferred_element_type=jnp.float32)
    dmixing = jnp.stack(
        [
            jnp.sum(dmixed * prob[0][None], axis=(1, 2)),
            jnp.sum(dmixed * prob[1][None], axis=(1, 2)),
        ],
        axis=-1,
    )
    dprob = (
        mixing_g[0][:, None, None] * dmixed[0][None] + mixing_g[1][:, None, None] * dmixed[1][None]
    )
    dconv = prob * (dprob - jnp.sum(prob * dprob, axis=-1, keepdims=True))
    dkernel = kernel_grads(dconv, logits, kernel_g.shape[1], kernel_g.shape[2])
    dlogits = convolve_back(dconv, kernel_g) * mask_ext * score_scale
    dquery = jnp.einsum(
        "hqk,khd->qhd",
        dlogits,
        key_g.astype(jnp.float32),
        precision=HIGHEST,
        preferred_element_type=jnp.float32,
    )
    dkey = jnp.einsum(
        "hqk,qhd->khd",
        dlogits,
        query_g.astype(jnp.float32),
        precision=HIGHEST,
        preferred_element_type=jnp.float32,
    )
    return (dquery, dkey, dvalue, dkernel, dmixing)


def rms_scale(values):
    return lax.rsqrt(jnp.mean(values * values, axis=-1, keepdims=True) + EPS)


def norm_back(grad_out, values, inv_scale, gain):
    scaled_grad = grad_out * gain
    inner = jnp.mean(scaled_grad * values, axis=-1, keepdims=True)
    return inv_scale * scaled_grad - values * inv_scale**3 * inner


def on_device(
    inputs,
    segment_ids,
    valid_mask,
    input_weight,
    output_weight,
    conv_kernel,
    head_mix,
    first_gain,
    second_gain,
    group_gain,
    gate_weight,
    up_weight,
    down_weight,
    cotangent,
):
    tokens = inputs.shape[1]
    model_width = inputs.shape[2]
    head_count = conv_kernel.shape[0]
    head_dim = model_width // head_count
    groups = head_mix.shape[0]
    rim_rows = conv_kernel.shape[1] - 1
    half_span = conv_kernel.shape[2] // 2
    window = REACH * tokens
    score_scale = head_dim ** (-0.5)
    seq_rank = lax.axis_index("seq")
    row_start = seq_rank * tokens
    window_start = row_start - (REACH - 1) * tokens
    resid_in = inputs[0].astype(jnp.float32)
    grad_out = cotangent[0].astype(jnp.float32)
    offset = window + half_span
    segment_pad = jnp.concatenate(
        [jnp.full((offset,), -1, jnp.int32), segment_ids[0], jnp.full((half_span,), -1, jnp.int32)]
    )
    valid_pad = jnp.concatenate(
        [jnp.zeros((offset,), jnp.int32), valid_mask[0], jnp.zeros((half_span,), jnp.int32)]
    )
    query_pos = row_start - rim_rows + jnp.arange(tokens + rim_rows, dtype=jnp.int32)
    key_pos = window_start - half_span + jnp.arange(window + 2 * half_span, dtype=jnp.int32)
    query_seg = lax.dynamic_slice_in_dim(
        segment_pad, row_start - rim_rows + offset, tokens + rim_rows
    )
    key_seg = lax.dynamic_slice_in_dim(
        segment_pad, window_start - half_span + offset, window + 2 * half_span
    )
    query_live = lax.dynamic_slice_in_dim(
        valid_pad, row_start - rim_rows + offset, tokens + rim_rows
    )
    key_live = lax.dynamic_slice_in_dim(
        valid_pad, window_start - half_span + offset, window + 2 * half_span
    )
    mask_ext = (
        (query_seg[:, None] == key_seg[None, :])
        & (key_pos[None, :] <= query_pos[:, None])
        & (query_live[:, None] > 0)
        & (key_live[None, :] > 0)
    ).astype(jnp.float32)
    mask_own = mask_ext[rim_rows:, half_span : half_span + window]
    row_valid = query_live[rim_rows:].astype(jnp.float32)[:, None]
    full_input, full_output = (
        lax.all_gather(input_weight, "seq", axis=0, tiled=True),
        lax.all_gather(output_weight, "seq", axis=0, tiled=True),
    )
    first_scale = rms_scale(resid_in)
    normed_in = (resid_in * first_scale * first_gain).astype(jnp.bfloat16)
    projected = jnp.dot(normed_in, full_input, preferred_element_type=jnp.float32).astype(
        jnp.bfloat16
    )
    query = projected[:, :model_width]
    keys_values = projected[:, model_width:]
    query_rim = from_behind(query[tokens - rim_rows :], "seq", 1)
    query_ext = jnp.concatenate([query_rim, query], axis=0)
    pieces = [keys_values]
    for distance in range(1, REACH):
        pieces.append(from_behind(keys_values, "seq", distance))
    window_rows = jnp.concatenate(pieces[::-1], axis=0)
    key_ext = jnp.pad(window_rows[:, :model_width], ((half_span, half_span), (0, 0)))
    value_window = window_rows[:, model_width:]

    def split_heads(values):
        return values.reshape(values.shape[0], groups, 2, head_dim).transpose(1, 0, 2, 3)

    def merge_heads(values):
        return values.transpose(1, 0, 2, 3).reshape(values.shape[1], model_width)

    query_groups = split_heads(query_ext)
    key_groups = split_heads(key_ext)
    value_groups = split_heads(value_window)
    kernel_groups = conv_kernel.reshape(groups, 2, conv_kernel.shape[1], conv_kernel.shape[2])
    result_groups, lse_groups = lax.map(
        lambda operands: attend_group(operands, mask_ext, mask_own, row_valid, score_scale),
        (query_groups, key_groups, value_groups, kernel_groups, head_mix),
    )
    attended = merge_heads(result_groups)
    shaped = attended.reshape(tokens, head_count, head_dim)
    centred = shaped - jnp.mean(shaped, axis=-1, keepdims=True)
    inv_std = lax.rsqrt(jnp.mean(centred * centred, axis=-1, keepdims=True) + EPS)
    unit_heads = centred * inv_std
    unit = unit_heads.reshape(tokens, model_width)
    normed = (unit * group_gain).astype(jnp.bfloat16)
    branch = jnp.dot(normed, full_output, preferred_element_type=jnp.float32)
    resid = resid_in + row_valid * branch
    second_scale = rms_scale(resid)
    normed_mid = (resid * second_scale * second_gain).astype(jnp.bfloat16)
    dmlp = (row_valid * grad_out).astype(jnp.bfloat16)
    contract_rows = (((0,), (0,)), ((), ()))
    inputs_all = lax.all_gather(normed_mid, "seq", axis=0, tiled=True)
    gate = jnp.dot(inputs_all, gate_weight, preferred_element_type=jnp.float32)
    up_proj = jnp.dot(inputs_all, up_weight, preferred_element_type=jnp.float32)
    hidden = (jax.nn.silu(gate) * up_proj).astype(jnp.bfloat16)
    mlp = lax.psum_scatter(
        jnp.dot(hidden, down_weight, preferred_element_type=jnp.float32).astype(jnp.bfloat16),
        "seq",
        scatter_dimension=0,
        tiled=True,
    ).astype(jnp.float32)
    result = resid + row_valid * mlp
    dmlp_all = lax.all_gather(dmlp, "seq", axis=0, tiled=True)
    dhidden = jnp.dot(dmlp_all, down_weight.T, preferred_element_type=jnp.float32)
    sigmoid_gate = jax.nn.sigmoid(gate)
    gate_grad = (dhidden * up_proj * sigmoid_gate * (1.0 + gate * (1.0 - sigmoid_gate))).astype(
        jnp.bfloat16
    )
    up_grad = (dhidden * gate * sigmoid_gate).astype(jnp.bfloat16)
    grad_down = lax.dot_general(hidden, dmlp_all, contract_rows, preferred_element_type=jnp.float32)
    grad_gate = lax.dot_general(
        inputs_all, gate_grad, contract_rows, preferred_element_type=jnp.float32
    )
    grad_up = lax.dot_general(
        inputs_all, up_grad, contract_rows, preferred_element_type=jnp.float32
    )
    dmid = lax.psum_scatter(
        (
            jnp.dot(gate_grad, gate_weight.T, preferred_element_type=jnp.float32)
            + jnp.dot(up_grad, up_weight.T, preferred_element_type=jnp.float32)
        ).astype(jnp.bfloat16),
        "seq",
        scatter_dimension=0,
        tiled=True,
    ).astype(jnp.float32)
    second_part = jnp.sum(dmid * resid * second_scale, axis=0)
    dresid = grad_out + norm_back(dmid, resid, second_scale, second_gain)
    dbranch = (row_valid * dresid).astype(jnp.bfloat16)
    whole_output_grad = lax.dot_general(
        normed, dbranch, contract_rows, preferred_element_type=jnp.float32
    )
    dnormed = jnp.dot(dbranch, full_output.T, preferred_element_type=jnp.float32)
    group_part = jnp.sum(dnormed * unit, axis=0)
    dunit = (dnormed * group_gain).reshape(tokens, head_count, head_dim)
    dshaped = inv_std * (
        dunit
        - jnp.mean(dunit, axis=-1, keepdims=True)
        - unit_heads * jnp.mean(dunit * unit_heads, axis=-1, keepdims=True)
    )
    dattended = dshaped.reshape(tokens, model_width).astype(jnp.bfloat16)
    dquery_g, dkey_g, dvalue_g, dkernel_g, dmixing = lax.map(
        lambda operands: attend_group_back(operands, mask_ext, mask_own, score_scale),
        (
            query_groups,
            key_groups,
            value_groups,
            kernel_groups,
            head_mix,
            split_heads(dattended),
            lse_groups,
        ),
    )
    dquery_ext = merge_heads(dquery_g)
    dkey_window = merge_heads(dkey_g)[half_span : half_span + window]
    dvalue_window = merge_heads(dvalue_g)
    dpair_window = jnp.concatenate([dkey_window, dvalue_window], axis=1)
    dpair = dpair_window[(REACH - 1) * tokens :]
    for distance in range(1, REACH):
        block_first = (REACH - 1 - distance) * tokens
        dpair = dpair + from_behind(
            dpair_window[block_first : block_first + tokens].astype(jnp.bfloat16), "seq", -distance
        ).astype(jnp.float32)
    rim_grad = from_behind(dquery_ext[:rim_rows], "seq", -1)
    dquery_own = dquery_ext[rim_rows:]
    dquery_own = jnp.concatenate(
        [dquery_own[: tokens - rim_rows], dquery_own[tokens - rim_rows :] + rim_grad], axis=0
    )
    dprojected = jnp.concatenate([dquery_own, dpair], axis=1).astype(jnp.bfloat16)
    whole_input_grad = lax.dot_general(
        normed_in, dprojected, contract_rows, preferred_element_type=jnp.float32
    )
    dnormin = jnp.dot(dprojected, full_input.T, preferred_element_type=jnp.float32)
    first_part = jnp.sum(dnormin * resid_in * first_scale, axis=0)
    grad_in = dresid + norm_back(dnormin, resid_in, first_scale, first_gain)
    input_shard, output_shard = (
        lax.psum_scatter(
            whole_input_grad.astype(jnp.bfloat16), "seq", scatter_dimension=0, tiled=True
        ).astype(jnp.float32),
        lax.psum_scatter(
            whole_output_grad.astype(jnp.bfloat16), "seq", scatter_dimension=0, tiled=True
        ).astype(jnp.float32),
    )
    kernel_part = dkernel_g.reshape(head_count, conv_kernel.shape[1], conv_kernel.shape[2])
    grad_kernel, grad_mix, grad_first, grad_second, grad_group = lax.psum(
        (kernel_part, dmixing, first_part, second_part, group_part), ("rep", "seq")
    )
    grad_input_w, grad_output_w, grad_gate, grad_up, grad_down = (
        lax.psum(input_shard.astype(jnp.bfloat16), "rep").astype(jnp.float32),
        lax.psum(output_shard.astype(jnp.bfloat16), "rep").astype(jnp.float32),
        lax.psum(grad_gate.astype(jnp.bfloat16), "rep").astype(jnp.float32),
        lax.psum(grad_up.astype(jnp.bfloat16), "rep").astype(jnp.float32),
        lax.psum(grad_down.astype(jnp.bfloat16), "rep").astype(jnp.float32),
    )
    return (
        result.astype(jnp.bfloat16)[None],
        grad_in.astype(jnp.bfloat16)[None],
        grad_input_w,
        grad_output_w,
        grad_kernel,
        grad_mix,
        grad_first,
        grad_second,
        grad_group,
        grad_gate,
        grad_up,
        grad_down,
    )


def solution(mesh):
    in_specs = (
        P("rep", "seq", None),
        P("rep", None),
        P("rep", None),
        P("seq", None),
        P("seq", None),
        P(),
        P(),
        P(),
        P(),
        P(),
        P(None, "seq"),
        P(None, "seq"),
        P("seq", None),
        P("rep", "seq", None),
    )
    out_specs = (
        P("rep", "seq", None),
        P("rep", "seq", None),
        P("seq", None),
        P("seq", None),
        P(),
        P(),
        P(),
        P(),
        P(),
        P(None, "seq"),
        P(None, "seq"),
        P("seq", None),
    )
    return jax.shard_map(
        on_device, mesh=mesh, in_specs=in_specs, out_specs=out_specs, check_vma=False
    )
```

profile of v0, /device:TPU:0, one launch (start us, length us, event | category | flops | bytes accessed | tf_op | source)
XLA Modules:
  0.0 4016.5 jit_solution(8021908718773649853)
XLA Ops:
  9.3 132.8 %all-gather.5.cloned.1.call-done = bf16[1536,4608]{1,0:T(8,128)(2,1)} async-done(((bf16[192,4608]{1,0:T(8,128)(2,1)}), bf16[1536,4608]{1,0:T(8,128)(2,1)}) %all-gather.5.cloned.1.call-update) | async-done | bytes 14155792 | tf_op jit(solution)/shard_map/all_gather | solution.py:209
  178.6 39.8 collective-permute-done.1
  218.4 47.0 %collective-permute-done = bf16[256,3072]{1,0:T(8,128)(2,1)} collective-permute-done((bf16[256,3072]{1,0:T(8,128)(2,1)}, bf16[256,3072]{1,0:T(8,128)(2,1)}, u32[]{:S(2)}, u32[]{:S(2)}) %collective-permute-start) | collective-permute-done | bytes 1572896 | tf_op jit(solution)/shard_map/ppermute | solution.py:14
  286.9 341.3 %while.34 = (s32[]{:T(128)}, f32[8,256,2,96]{1,3,2,0:T(8,128)S(1)}, f32[8,2,256,1]{2,1,3,0:T(2,128)}, bf16[8,1024,2,96]{1,3,2,0:T(8,128)(2,1)}, f32[8,2,2]{2,1,0...) while((s32[]{:T(128)}, f32[8,256,2,96]{1,3,2,0:T(8,128)S(1)}, ...), condition=%wide.region_4.5_spmd.clone, body=%wide.region_1.4_spmd.clone.sunk | while | flops 281692032 | bytes 160720624 | solution.py:238
  652.1 102.0 %all-gather.9.cloned.1.call-done = bf16[2048,1536]{1,0:T(8,128)(2,1)} async-done(((bf16[256,1536]{1,0:T(8,128)(2,1)}), bf16[2048,1536]{1,0:T(8,128)(2,1)}) %all-gather.9.cloned.1.call-update) | async-done | bytes 6291472 | tf_op jit(solution)/shard_map/all_gather | solution.py:255
  767.9 51.8 %all-gather.11.cloned.1.call-done = bf16[2048,1536]{1,0:T(8,128)(2,1)} async-done(((bf16[256,1536]{1,0:T(8,128)(2,1)}), bf16[2048,1536]{1,0:T(8,128)(2,1)}) %all-gather.11.cloned.1.call-update) | async-done | bytes 6291472 | tf_op jit(solution)/shard_map/all_gather | solution.py:266
  848.9 61.1 %reduce-scatter.7.cloned.1.call-done = bf16[256,1536]{1,0:T(8,128)(2,1)} async-done(((bf16[2048,1536]{1,0:T(8,128)(2,1)}), bf16[256,1536]{1,0:T(8,128)(2,1)}) %reduce-scatter.7.cloned.1.call-update) | async-done | bytes 786448 | tf_op jit(solution)/shard_map/reduce_scatter | solution.py:280
  912.2 68.2 %reduce-scatter.5.cloned.1.call-done = bf16[256,1536]{1,0:T(8,128)(2,1)} async-done(((bf16[2048,1536]{1,0:T(8,128)(2,1)}), bf16[256,1536]{1,0:T(8,128)(2,1)}) %reduce-scatter.5.cloned.1.call-update) | async-done | bytes 786448 | tf_op jit(solution)/shard_map/reduce_scatter | solution.py:259
  1008.2 2550.7 %while.35 = (s32[]{:T(128)}, f32[8,261,2,96]{3,1,2,0:T(8,128)}, f32[8,1034,2,96]{1,3,2,0:T(8,128)}, f32[8,1024,2,96]{1,3,2,0:T(8,128)}, f32[8,2,6,11]{3,1,0,2:T(...) while((s32[]{:T(128)}, f32[8,261,2,96]{3,1,2,0:T(8,128)}, ...), condition=%wide.region_83.84_spmd.clone, body=%wide.region_13.83_spmd.clone.sunk | while | flops 1772737280 | bytes 370601792 | solution.py:304
  1041.3 36.7 multiply_reduce_fusion.77
  1163.3 124.6 %multiply_multiply_fusion.4 = f32[2,261,1034]{2,1,0:T(8,128)S(1)} fusion(f32[2,256,1024]{2,1,0:T(8,128)} %get-tuple-element.1464, f32[261,1034]{1,0:T(8,128)} %fusion.360, f32[2]{0:T(128)} %get-tuple-element.1396, f32[2]{0:T(128)} %get-tuple-element.1397, f32[2]{0:T(128)} %get-tuple-element.1398, f32[2]{0:T(128)} %get-tuple-element.1399, ...), kind=kLoop, calls=%fused_computation.436.clone.1 | loop fusion | flops 71786448 | bytes 5336168 | tf_op jit(solution)/shard_map/while/body/eval_jaxpr/mul | solution.py:121
  1478.6 124.6 %multiply_multiply_fusion.4 = f32[2,261,1034]{2,1,0:T(8,128)S(1)} fusion(f32[2,256,1024]{2,1,0:T(8,128)} %get-tuple-element.1464, f32[261,1034]{1,0:T(8,128)} %fusion.360, f32[2]{0:T(128)} %get-tuple-element.1396, f32[2]{0:T(128)} %get-tuple-element.1397, f32[2]{0:T(128)} %get-tuple-element.1398, f32[2]{0:T(128)} %get-tuple-element.1399, ...), kind=kLoop, calls=%fused_computation.436.clone.1 | loop fusion | flops 71786448 | bytes 5336168 | tf_op jit(solution)/shard_map/while/body/eval_jaxpr/mul | solution.py:121
  1671.8 36.7 multiply_reduce_fusion.77
  1793.8 124.6 %multiply_multiply_fusion.4 = f32[2,261,1034]{2,1,0:T(8,128)S(1)} fusion(f32[2,256,1024]{2,1,0:T(8,128)} %get-tuple-element.1464, f32[261,1034]{1,0:T(8,128)} %fusion.360, f32[2]{0:T(128)} %get-tuple-element.1396, f32[2]{0:T(128)} %get-tuple-element.1397, f32[2]{0:T(128)} %get-tuple-element.1398, f32[2]{0:T(128)} %get-tuple-element.1399, ...), kind=kLoop, calls=%fused_computation.436.clone.1 | loop fusion | flops 71786448 | bytes 5336168 | tf_op jit(solution)/shard_map/while/body/eval_jaxpr/mul | solution.py:121
  2109.1 124.6 %multiply_multiply_fusion.4 = f32[2,261,1034]{2,1,0:T(8,128)S(1)} fusion(f32[2,256,1024]{2,1,0:T(8,128)} %get-tuple-element.1464, f32[261,1034]{1,0:T(8,128)} %fusion.360, f32[2]{0:T(128)} %get-tuple-element.1396, f32[2]{0:T(128)} %get-tuple-element.1397, f32[2]{0:T(128)} %get-tuple-element.1398, f32[2]{0:T(128)} %get-tuple-element.1399, ...), kind=kLoop, calls=%fused_computation.436.clone.1 | loop fusion | flops 71786448 | bytes 5336168 | tf_op jit(solution)/shard_map/while/body/eval_jaxpr/mul | solution.py:121
  2424.4 124.6 %multiply_multiply_fusion.4 = f32[2,261,1034]{2,1,0:T(8,128)S(1)} fusion(f32[2,256,1024]{2,1,0:T(8,128)} %get-tuple-element.1464, f32[261,1034]{1,0:T(8,128)} %fusion.360, f32[2]{0:T(128)} %get-tuple-element.1396, f32[2]{0:T(128)} %get-tuple-element.1397, f32[2]{0:T(128)} %get-tuple-element.1398, f32[2]{0:T(128)} %get-tuple-element.1399, ...), kind=kLoop, calls=%fused_computation.436.clone.1 | loop fusion | flops 71786448 | bytes 5336168 | tf_op jit(solution)/shard_map/while/body/eval_jaxpr/mul | solution.py:121
  2617.6 36.7 multiply_reduce_fusion.77
  2739.6 124.6 %multiply_multiply_fusion.4 = f32[2,261,1034]{2,1,0:T(8,128)S(1)} fusion(f32[2,256,1024]{2,1,0:T(8,128)} %get-tuple-element.1464, f32[261,1034]{1,0:T(8,128)} %fusion.360, f32[2]{0:T(128)} %get-tuple-element.1396, f32[2]{0:T(128)} %get-tuple-element.1397, f32[2]{0:T(128)} %get-tuple-element.1398, f32[2]{0:T(128)} %get-tuple-element.1399, ...), kind=kLoop, calls=%fused_computation.436.clone.1 | loop fusion | flops 71786448 | bytes 5336168 | tf_op jit(solution)/shard_map/while/body/eval_jaxpr/mul | solution.py:121
  3054.9 124.6 %multiply_multiply_fusion.4 = f32[2,261,1034]{2,1,0:T(8,128)S(1)} fusion(f32[2,256,1024]{2,1,0:T(8,128)} %get-tuple-element.1464, f32[261,1034]{1,0:T(8,128)} %fusion.360, f32[2]{0:T(128)} %get-tuple-element.1396, f32[2]{0:T(128)} %get-tuple-element.1397, f32[2]{0:T(128)} %get-tuple-element.1398, f32[2]{0:T(128)} %get-tuple-element.1399, ...), kind=kLoop, calls=%fused_computation.436.clone.1 | loop fusion | flops 71786448 | bytes 5336168 | tf_op jit(solution)/shard_map/while/body/eval_jaxpr/mul | solution.py:121
  3370.2 124.6 %multiply_multiply_fusion.4 = f32[2,261,1034]{2,1,0:T(8,128)S(1)} fusion(f32[2,256,1024]{2,1,0:T(8,128)} %get-tuple-element.1464, f32[261,1034]{1,0:T(8,128)} %fusion.360, f32[2]{0:T(128)} %get-tuple-element.1396, f32[2]{0:T(128)} %get-tuple-element.1397, f32[2]{0:T(128)} %get-tuple-element.1398, f32[2]{0:T(128)} %get-tuple-element.1399, ...), kind=kLoop, calls=%fused_computation.436.clone.1 | loop fusion | flops 71786448 | bytes 5336168 | tf_op jit(solution)/shard_map/while/body/eval_jaxpr/mul | solution.py:121
  3620.5 38.8 collective-permute-done.6
  3693.2 147.7 %reduce-scatter.9.cloned.1.call-done = bf16[192,4608]{1,0:T(8,128)(2,1)} async-done(((bf16[1536,4608]{1,0:T(8,128)(2,1)}), bf16[192,4608]{1,0:T(8,128)(2,1)}) %reduce-scatter.9.cloned.1.call-update) | async-done | bytes 1769488 | tf_op jit(solution)/shard_map/reduce_scatter | solution.py:339
  3853.7 40.1 all-reduce.2
  3898.0 100.9 %all-reduce.6.cloned.1.call-done = (bf16[192,4608]{1,0:T(8,128)(2,1)}, bf16[192,1536]{1,0:T(8,128)(2,1)}, bf16[1536,512]{1,0:T(8,128)(2,1)}, bf16[1536,512]{1,0:T(8,128)(2,1)}, bf16[512,1536]{1,0:T(8,128)(2,1)}) async-done(((bf16[192,4608]{1,0:T(8,128)(2,1)}, bf16[192,1536]{1,0:T(8,128)(2,1)}, bf16[1536,512]{1,0:T(8,128)(2,1)}, bf16[1536,512]{1,0:T(8,128)(2,1)}, bf16[512,1536]{1,0:T(8,128)(2,1)}), ...) | async-done | bytes 7077904 | tf_op jit(solution)/shard_map/psum | solution.py:351
  (1999 shorter events, 2029.6 us)
Async XLA Ops:
  7.2 812.5 %copy-start = (bf16[512,1536]{1,0:T(8,128)(2,1)S(1)}, bf16[512,1536]{1,0:T(8,128)(2,1)}, u32[]{:S(2)}) copy-start(bf16[512,1536]{1,0:T(8,128)(2,1)} %param.30) | copy-start | bytes 4718596
  7.2 134.9 %copy-start.64 = (f32[1536]{0:T(1024)S(1)}, f32[1536]{0:T(1024)}, u32[]{:S(2)}) copy-start(f32[1536]{0:T(1024)} %param.25) | copy-start | bytes 18436
  7.2 134.8 %all-gather.5.cloned.1.call-start = ((), (), s32[]{:S(2)}) async-start(), calls=%async_computation.4 | async-start | bytes 15925248 | tf_op jit(solution)/shard_map/all_gather | solution.py:209
  8.0 634.8 %all-gather.7.cloned.1.call-start = ((), (), s32[]{:S(2)}) async-start(), calls=%async_computation.5 | async-start | bytes 5308416 | tf_op jit(solution)/shard_map/all_gather | solution.py:210
  9.3 142.0 %copy-start.72 = (f32[256]{0:T(256)}, f32[256]{0:T(256)S(1)}, u32[]{:S(2)}) copy-start(f32[256]{0:T(256)S(1)} %get-tuple-element.869) | copy-start | bytes 3076
  154.1 24.5 collective-permute-start.2
  157.4 61.1 %collective-permute-start.1 = (bf16[256,3072]{1,0:T(8,128)(2,1)}, bf16[256,3072]{1,0:T(8,128)(2,1)}, u32[]{:S(2)}, u32[]{:S(2)}) collective-permute-start(bf16[256,3072]{1,0:T(8,128)(2,1)} %slice.2477), channel_id=1, source_target_pairs={{0,2},{1,3},{2,4},{3,5},{4,6},{5,7},{8,10},{9,11},{10,12},{11,13},... | collective-permute-start | bytes 4718600 | tf_op jit(solution)/shard_map/ppermute | solution.py:14
  159.8 105.6 %collective-permute-start = (bf16[256,3072]{1,0:T(8,128)(2,1)}, bf16[256,3072]{1,0:T(8,128)(2,1)}, u32[]{:S(2)}, u32[]{:S(2)}) collective-permute-start(bf16[256,3072]{1,0:T(8,128)(2,1)} %slice.2477), channel_id=1, source_target_pairs={{0,3},{1,4},{2,5},{3,6},{4,7},{8,11},{9,12},{10,13},{11,14},{12,15... | collective-permute-start | bytes 4718600 | tf_op jit(solution)/shard_map/ppermute | solution.py:14
  162.3 591.8 %all-gather.9.cloned.1.call-start = ((), (), s32[]{:S(2)}) async-start(), calls=%async_computation.6 | async-start | bytes 7077888 | tf_op jit(solution)/shard_map/all_gather | solution.py:255
  165.4 3.6 collective-permute-start.3
  649.5 170.1 %all-gather.11.cloned.1.call-start = ((), (), s32[]{:S(2)}) async-start(), calls=%async_computation.8 | async-start | bytes 7077888 | tf_op jit(solution)/shard_map/all_gather | solution.py:266
  651.8 258.2 %reduce-scatter.7.cloned.1.call-start = ((), (), s32[]{:S(2)}) async-start(), calls=%async_computation.9 | async-start | bytes 7077888 | tf_op jit(solution)/shard_map/reduce_scatter | solution.py:280
  841.4 139.0 %reduce-scatter.5.cloned.1.call-start = ((), (), s32[]{:S(2)}) async-start(), calls=%async_computation.7 | async-start | bytes 7077888 | tf_op jit(solution)/shard_map/reduce_scatter | solution.py:259
  848.4 2844.7 %reduce-scatter.11.cloned.1.call-start = ((), (), s32[]{:S(2)}) async-start(), calls=%async_computation.11 | async-start | bytes 5308416 | tf_op jit(solution)/shard_map/reduce_scatter | solution.py:342
  1008.2 2832.7 %reduce-scatter.9.cloned.1.call-start = ((), (), s32[]{:S(2)}) async-start(), calls=%async_computation.10 | async-start | bytes 15925248 | tf_op jit(solution)/shard_map/reduce_scatter | solution.py:339
  3579.2 12.6 collective-permute-start.5
  3580.5 40.1 collective-permute-start.7
  3581.8 77.6 %collective-permute-start.6 = (bf16[256,3072]{0,1:T(8,128)(2,1)}, bf16[256,3072]{0,1:T(8,128)(2,1)}, u32[]{:S(2)}, u32[]{:S(2)}) collective-permute-start(bf16[256,3072]{0,1:T(8,128)(2,1)} %get-tuple-element.859), channel_id=1, source_target_pairs={{2,0},{3,1},{4,2},{5,3},{6,4},{7,5},{10,8},{11,9},{12,10},{13,11},... | collective-permute-start | bytes 4718600 | tf_op jit(solution)/shard_map/ppermute | solution.py:14
  3587.7 3.8 collective-permute-start.4
  3591.7 71.6 %copy-start.15 = (bf16[1,256,1536]{2,1,0:T(8,128)(2,1)S(1)}, bf16[1,256,1536]{2,1,0:T(8,128)(2,1)}, u32[]{:S(2)}) copy-start(bf16[1,256,1536]{2,1,0:T(8,128)(2,1)} %param.18) | copy-start | bytes 2359300
  3591.8 71.5 %copy-start.20 = (bf16[251,8,2,96]{0,3,2,1:T(8,128)(2,1)S(1)}, bf16[251,8,2,96]{0,3,2,1:T(8,128)(2,1)}, u32[]{:S(2)}) copy-start(bf16[251,8,2,96]{0,3,2,1:T(8,128)(2,1)} %slice.3701) | copy-start | bytes 2313220
  3591.8 71.5 %copy-start.65 = (f32[1536]{0:T(1024)S(1)}, f32[1536]{0:T(1024)}, u32[]{:S(2)}) copy-start(f32[1536]{0:T(1024)} %param.25) | copy-start | bytes 18436
  3591.8 71.5 %copy-start.73 = (f32[256]{0:T(256)S(1)}, f32[256]{0:T(256)}, u32[]{:S(2)}) copy-start(f32[256]{0:T(256)} %copy-done.72) | copy-start | bytes 3076
  3672.5 326.4 %all-reduce.6.cloned.1.call-start = ((), (), s32[]{:S(2)}) async-start(), calls=%async_computation.12 | async-start | bytes 14155776 | tf_op jit(solution)/shard_map/psum | solution.py:351
  (417 other events, 4098.7 us)
Sparse Core Ops, SparseCore 0:
  9.7 132.3 all-gather.4
  162.4 82.5 all-gather.6
  649.7 104.4 all-gather.8
  756.2 63.4 all-gather.10
  841.5 68.4 reduce-scatter.6
  912.1 68.1 reduce-scatter.4
  1008.3 53.3 reduce-scatter.10
  3672.7 168.1 reduce-scatter.8
  3846.3 152.5 all-reduce.5
where the time goes:
time: 4040 us; the launch traced here: 4020 us
  other arithmetic  2010 us (50%)
  local copies, waits for them, and re-layouts  853 us (21%)
  waiting for transfers between devices  821 us (20%)
  matrix products  225 us (6%)
    mul x8, other arithmetic, attend_group_back(): dlogits = convolve_back(dconv, kernel_g) * mask_ext * score_scale  997 us
    another operation x576, local copies, waits for them, and re-layouts, kernel_grads(): entries.append(jnp.stack(line_sums, axis=-1))  678 us
    reduce_sum x32, other arithmetic, kernel_grads(): line_sums.append(jnp.sum(grads * window_part, axis=(1, 2)))  334 us
    reduce_sum x8, other arithmetic, attend_group_back(): dconv = prob * (dprob - jnp.sum(prob * dprob, axis=-1, keepdims=True))  294 us
    reduce_max x8, other arithmetic, attend_group(): peak = jnp.max(jnp.where(allowed, conv, -1e+30), axis=-1, keepdims=True)  277 us
    ppermute x8, waiting for transfers between devices, from_behind(): return lax.ppermute(x, axis, pairs)  155 us
    reduce_scatter x1, waiting for transfers between devices, on_device(): lax.psum_scatter(whole_input_grad.astype(jnp.bfloat16), 'seq', scatter_di...  148 us
    all_gather x1, waiting for transfers between devices, on_device(): lax.all_gather(input_weight, 'seq', axis=0, tiled=True)  133 us
  transfers between devices with their start and end apart: 17, of which 12 were waited for; matrix products, arithmetic and copies ran while one was open for 74% of the time, Pallas kernels for 0%

commit v1 on v0

--- a/solution.py
+++ b/solution.py
@@ -162,6 +162,19 @@
     down_weight,
     cotangent,
 ):
+
+    def _guide_surface(point, mesh_name):
+        extent = lax.psum(1, mesh_name)
+        earlier = point
+        items = [earlier]
+        mixed_arr = [(dev_j - 1, dev_j) for dev_j in range(1, extent)] + [(extent - 1, 0)]
+        for _ in [*range(extent - 1)]:
+            earlier = lax.ppermute(earlier, mesh_name, mixed_arr)
+            items += [earlier]
+        g_now = jnp.concatenate([*reversed(items)], 0)
+        b_next = lax.axis_index(mesh_name)
+        return jnp.roll(g_now, (b_next + 1) * earlier.shape[0], 0)
+
     tokens = inputs.shape[1]
     model_width = inputs.shape[2]
     head_count = conv_kernel.shape[0]
@@ -252,7 +265,7 @@
     normed_mid = (resid * second_scale * second_gain).astype(jnp.bfloat16)
     dmlp = (row_valid * grad_out).astype(jnp.bfloat16)
     contract_rows = (((0,), (0,)), ((), ()))
-    inputs_all = lax.all_gather(normed_mid, "seq", axis=0, tiled=True)
+    inputs_all = _guide_surface(normed_mid, "seq")
     gate = jnp.dot(inputs_all, gate_weight, preferred_element_type=jnp.float32)
     up_proj = jnp.dot(inputs_all, up_weight, preferred_element_type=jnp.float32)
     hidden = (jax.nn.silu(gate) * up_proj).astype(jnp.bfloat16)

time: 4040 us -> 2980 us (0.74)
  other arithmetic: 2010 us -> 1370 us
  local copies, waits for them, and re-layouts: 853 us -> 441 us
  starting transfers between devices: 16.5 us -> 118 us
  waiting for transfers between devices: 821 us -> 723 us
    mul x8, other arithmetic: 997 us -> 356 us  [attend_group_back(): dlogits = convolve_back(dconv, kernel_g) * mask_ext * score_scale]
    another operation x576, local copies, waits for them, and re-layouts: 678 us -> 235 us  [kernel_grads(): entries.append(jnp.stack(line_sums, axis=-1))]
    all_gather x1 -> x0, waiting for transfers between devices: 102 us -> none  [on_device(): inputs_all = lax.all_gather(normed_mid, 'seq', axis=0, tiled=True)]
    ppermute x0 -> x7, starting transfers between devices: none -> 101 us  [_guide_surface(): earlier = lax.ppermute(earlier, mesh_name, mixed_arr)]
    all_gather x1, waiting for transfers between devices: 51.8 us -> 0.01 us  [on_device(): dmlp_all = lax.all_gather(dmlp, 'seq', axis=0, tiled=True)]
  transfers between devices with their start and end apart: 17 -> 23, of which waited for: 12 -> 17; matrix products, arithmetic and copies ran while one was open for 74% -> 66% of each run, Pallas kernels for 0% -> 0%
where the time goes in v1:
time: 2980 us; the launch traced here: 2970 us
  other arithmetic  1370 us (46%)
  waiting for transfers between devices  723 us (24%)
  local copies, waits for them, and re-layouts  441 us (15%)
  matrix products  246 us (8%)
  starting transfers between devices  118 us (4%)
  blocking collectives  40.1 us (1%)
    mul x8, other arithmetic, attend_group_back(): dlogits = convolve_back(dconv, kernel_g) * mask_ext * score_scale  356 us
    reduce_sum x32, other arithmetic, kernel_grads(): line_sums.append(jnp.sum(grads * window_part, axis=(1, 2)))  335 us
    reduce_sum x8, other arithmetic, attend_group_back(): dconv = prob * (dprob - jnp.sum(prob * dprob, axis=-1, keepdims=True))  294 us
    reduce_max x8, other arithmetic, attend_group(): peak = jnp.max(jnp.where(allowed, conv, -1e+30), axis=-1, keepdims=True)  277 us
    another operation x576, local copies, waits for them, and re-layouts, kernel_grads(): entries.append(jnp.stack(line_sums, axis=-1))  235 us
    ppermute x8, waiting for transfers between devices, from_behind(): return lax.ppermute(x, axis, pairs)  160 us
    reduce_scatter x1, waiting for transfers between devices, on_device(): lax.psum_scatter(whole_input_grad.astype(jnp.bfloat16), 'seq', scatter_di...  157 us
    all_gather x1, waiting for transfers between devices, on_device(): lax.all_gather(input_weight, 'seq', axis=0, tiled=True)  132 us
  transfers between devices with their start and end apart: 23, of which 17 were waited for; matrix products, arithmetic and copies ran while one was open for 66% of the time, Pallas kernels for 0%

profile of v1, /device:TPU:0, one launch (start us, length us, event | category | flops | bytes accessed | tf_op | source)
XLA Modules:
  0.0 2971.2 jit_solution(3652721059938424560)
XLA Ops:
  9.7 132.3 %all-gather.4.cloned.1.call-done = bf16[1536,4608]{1,0:T(8,128)(2,1)} async-done(((bf16[192,4608]{1,0:T(8,128)(2,1)}), bf16[1536,4608]{1,0:T(8,128)(2,1)}) %all-gather.4.cloned.1.call-update) | async-done | bytes 14155792 | tf_op jit(solution)/shard_map/all_gather | solution.py:222
  175.5 46.3 %collective-permute-done = bf16[256,3072]{1,0:T(8,128)(2,1)} collective-permute-done((bf16[256,3072]{1,0:T(8,128)(2,1)}, bf16[256,3072]{1,0:T(8,128)(2,1)}, u32[]{:S(2)}, u32[]{:S(2)}) %collective-permute-start) | collective-permute-done | bytes 1572896 | tf_op jit(solution)/shard_map/ppermute | solution.py:14
  221.8 54.2 %collective-permute-done.1 = bf16[256,3072]{1,0:T(8,128)(2,1)} collective-permute-done((bf16[256,3072]{1,0:T(8,128)(2,1)}, bf16[256,3072]{1,0:T(8,128)(2,1)}, u32[]{:S(2)}, u32[]{:S(2)}) %collective-permute-start.1) | collective-permute-done | bytes 1572896 | tf_op jit(solution)/shard_map/ppermute | solution.py:14
  297.7 337.2 %while.34 = (s32[]{:T(128)}, f32[8,256,2,96]{1,3,2,0:T(8,128)}, f32[8,2,256,1]{2,1,3,0:T(2,128)}, bf16[8,1024,2,96]{1,3,2,0:T(8,128)(2,1)}, f32[8,2,2]{2,1,0:T(2...) while((s32[]{:T(128)}, f32[8,256,2,96]{1,3,2,0:T(8,128)}, ...), condition=%wide.region_4.5_spmd.clone, body=%wide.region_1.4_spmd.clone.sunk | while | flops 281692032 | bytes 160720112 | solution.py:251
  659.5 52.1 %collective-permute-start.4 = (bf16[256,1536]{1,0:T(8,128)(2,1)S(1)}, bf16[256,1536]{1,0:T(8,128)(2,1)S(1)}, u32[]{:S(2)}, u32[]{:S(2)}) collective-permute-start(bf16[256,1536]{1,0:T(8,128)(2,1)S(1)} %multiply_convert_fusion.5), channel_id=1, source_target_pairs={{0,1},{1,2},{2,3},{3,4},{4,5},{5,6},{6,7},{7,0},{8,9},{9,10},{10,1... | collective-permute-start | bytes 2359304 | tf_op jit(solution)/shard_map/ppermute | solution.py:172
  848.7 74.6 %reduce-scatter.7.cloned.1.call-done = bf16[256,1536]{1,0:T(8,128)(2,1)} async-done(((bf16[2048,1536]{1,0:T(8,128)(2,1)}), bf16[256,1536]{1,0:T(8,128)(2,1)}) %reduce-scatter.7.cloned.1.call-update) | async-done | bytes 786448 | tf_op jit(solution)/shard_map/reduce_scatter | solution.py:293
  925.4 68.2 %reduce-scatter.5.cloned.1.call-done = bf16[256,1536]{1,0:T(8,128)(2,1)} async-done(((bf16[2048,1536]{1,0:T(8,128)(2,1)}), bf16[256,1536]{1,0:T(8,128)(2,1)}) %reduce-scatter.5.cloned.1.call-update) | async-done | bytes 786448 | tf_op jit(solution)/shard_map/reduce_scatter | solution.py:272
  1023.1 1489.3 %while.35 = (s32[]{:T(128)}, f32[8,261,2,96]{3,1,2,0:T(8,128)}, f32[8,1034,2,96]{1,3,2,0:T(8,128)}, f32[8,1024,2,96]{1,3,2,0:T(8,128)}, f32[8,2,6,11]{3,1,0,2:T(...) while((s32[]{:T(128)}, f32[8,261,2,96]{3,1,2,0:T(8,128)}, ...), condition=%wide.region_83.84_spmd.clone, body=%wide.region_13.83_spmd.clone.sunk | while | flops 1772737280 | bytes 377415552 | solution.py:317
  1156.8 44.5 %multiply_multiply_fusion.4 = f32[2,261,1034]{2,1,0:T(8,128)} fusion(f32[2,256,1024]{2,1,0:T(8,128)S(1)} %copy-done.2, f32[261,1034]{1,0:T(8,128)} %fusion.373, f32[2]{0:T(128)S(1)} %get-tuple-element.1396, f32[2]{0:T(128)S(1)} %get-tuple-element.1397, f32[2]{0:T(128)S(1)} %get-tuple-element.1398, f32[2]{0:T(128)S(1)} %get-tuple-element.1399, ...), kind=kLoop, calls=%fused_computation.436.clone.1 | loop fusion | flops 71786448 | bytes 5336168 | tf_op jit(solution)/shard_map/while/body/eval_jaxpr/mul | solution.py:121
  1219.4 36.7 %multiply_reduce_fusion.77 = (f32[2,256]{1,0:T(2,128)S(1)}, f32[2,256,1024]{2,1,0:T(8,128)S(1)}) fusion(f32[256,1024]{1,0:T(8,128)} %get-tuple-element.1392, f32[2]{0:T(128)} %get-tuple-element.1393, f32[256,1024]{1,0:T(8,128)S(1)} %get-tuple-element.1394, f32[2]{0:T(128)} %get-tuple-element.1395, f32[2,256]{1,0:T(2,128)S(1)} %fusion.372, ...), kind=kLoop, calls=%fused_computation.507.clone.1 | loop fusion | flops 72351232 | bytes 142873120 | tf_op jit(solution)/shard_map/while/body/eval_jaxpr/reduce_sum | solution.py:119
  1342.0 44.5 %multiply_multiply_fusion.4 = f32[2,261,1034]{2,1,0:T(8,128)} fusion(f32[2,256,1024]{2,1,0:T(8,128)S(1)} %copy-done.2, f32[261,1034]{1,0:T(8,128)} %fusion.373, f32[2]{0:T(128)S(1)} %get-tuple-element.1396, f32[2]{0:T(128)S(1)} %get-tuple-element.1397, f32[2]{0:T(128)S(1)} %get-tuple-element.1398, f32[2]{0:T(128)S(1)} %get-tuple-element.1399, ...), kind=kLoop, calls=%fused_computation.436.clone.1 | loop fusion | flops 71786448 | bytes 5336168 | tf_op jit(solution)/shard_map/while/body/eval_jaxpr/mul | solution.py:121
  1527.1 44.5 %multiply_multiply_fusion.4 = f32[2,261,1034]{2,1,0:T(8,128)} fusion(f32[2,256,1024]{2,1,0:T(8,128)S(1)} %copy-done.2, f32[261,1034]{1,0:T(8,128)} %fusion.373, f32[2]{0:T(128)S(1)} %get-tuple-element.1396, f32[2]{0:T(128)S(1)} %get-tuple-element.1397, f32[2]{0:T(128)S(1)} %get-tuple-element.1398, f32[2]{0:T(128)S(1)} %get-tuple-element.1399, ...), kind=kLoop, calls=%fused_computation.436.clone.1 | loop fusion | flops 71786448 | bytes 5336168 | tf_op jit(solution)/shard_map/while/body/eval_jaxpr/mul | solution.py:121
  1712.3 44.5 %multiply_multiply_fusion.4 = f32[2,261,1034]{2,1,0:T(8,128)} fusion(f32[2,256,1024]{2,1,0:T(8,128)S(1)} %copy-done.2, f32[261,1034]{1,0:T(8,128)} %fusion.373, f32[2]{0:T(128)S(1)} %get-tuple-element.1396, f32[2]{0:T(128)S(1)} %get-tuple-element.1397, f32[2]{0:T(128)S(1)} %get-tuple-element.1398, f32[2]{0:T(128)S(1)} %get-tuple-element.1399, ...), kind=kLoop, calls=%fused_computation.436.clone.1 | loop fusion | flops 71786448 | bytes 5336168 | tf_op jit(solution)/shard_map/while/body/eval_jaxpr/mul | solution.py:121
  1775.0 36.7 %multiply_reduce_fusion.77 = (f32[2,256]{1,0:T(2,128)S(1)}, f32[2,256,1024]{2,1,0:T(8,128)S(1)}) fusion(f32[256,1024]{1,0:T(8,128)} %get-tuple-element.1392, f32[2]{0:T(128)} %get-tuple-element.1393, f32[256,1024]{1,0:T(8,128)S(1)} %get-tuple-element.1394, f32[2]{0:T(128)} %get-tuple-element.1395, f32[2,256]{1,0:T(2,128)S(1)} %fusion.372, ...), kind=kLoop, calls=%fused_computation.507.clone.1 | loop fusion | flops 72351232 | bytes 142873120 | tf_op jit(solution)/shard_map/while/body/eval_jaxpr/reduce_sum | solution.py:119
  1897.5 44.5 %multiply_multiply_fusion.4 = f32[2,261,1034]{2,1,0:T(8,128)} fusion(f32[2,256,1024]{2,1,0:T(8,128)S(1)} %copy-done.2, f32[261,1034]{1,0:T(8,128)} %fusion.373, f32[2]{0:T(128)S(1)} %get-tuple-element.1396, f32[2]{0:T(128)S(1)} %get-tuple-element.1397, f32[2]{0:T(128)S(1)} %get-tuple-element.1398, f32[2]{0:T(128)S(1)} %get-tuple-element.1399, ...), kind=kLoop, calls=%fused_computation.436.clone.1 | loop fusion | flops 71786448 | bytes 5336168 | tf_op jit(solution)/shard_map/while/body/eval_jaxpr/mul | solution.py:121
  2082.7 44.5 %multiply_multiply_fusion.4 = f32[2,261,1034]{2,1,0:T(8,128)} fusion(f32[2,256,1024]{2,1,0:T(8,128)S(1)} %copy-done.2, f32[261,1034]{1,0:T(8,128)} %fusion.373, f32[2]{0:T(128)S(1)} %get-tuple-element.1396, f32[2]{0:T(128)S(1)} %get-tuple-element.1397, f32[2]{0:T(128)S(1)} %get-tuple-element.1398, f32[2]{0:T(128)S(1)} %get-tuple-element.1399, ...), kind=kLoop, calls=%fused_computation.436.clone.1 | loop fusion | flops 71786448 | bytes 5336168 | tf_op jit(solution)/shard_map/while/body/eval_jaxpr/mul | solution.py:121
  2145.3 36.7 %multiply_reduce_fusion.77 = (f32[2,256]{1,0:T(2,128)S(1)}, f32[2,256,1024]{2,1,0:T(8,128)S(1)}) fusion(f32[256,1024]{1,0:T(8,128)} %get-tuple-element.1392, f32[2]{0:T(128)} %get-tuple-element.1393, f32[256,1024]{1,0:T(8,128)S(1)} %get-tuple-element.1394, f32[2]{0:T(128)} %get-tuple-element.1395, f32[2,256]{1,0:T(2,128)S(1)} %fusion.372, ...), kind=kLoop, calls=%fused_computation.507.clone.1 | loop fusion | flops 72351232 | bytes 142873120 | tf_op jit(solution)/shard_map/while/body/eval_jaxpr/reduce_sum | solution.py:119
  2267.9 44.5 %multiply_multiply_fusion.4 = f32[2,261,1034]{2,1,0:T(8,128)} fusion(f32[2,256,1024]{2,1,0:T(8,128)S(1)} %copy-done.2, f32[261,1034]{1,0:T(8,128)} %fusion.373, f32[2]{0:T(128)S(1)} %get-tuple-element.1396, f32[2]{0:T(128)S(1)} %get-tuple-element.1397, f32[2]{0:T(128)S(1)} %get-tuple-element.1398, f32[2]{0:T(128)S(1)} %get-tuple-element.1399, ...), kind=kLoop, calls=%fused_computation.436.clone.1 | loop fusion | flops 71786448 | bytes 5336168 | tf_op jit(solution)/shard_map/while/body/eval_jaxpr/mul | solution.py:121
  2330.5 36.7 %multiply_reduce_fusion.77 = (f32[2,256]{1,0:T(2,128)S(1)}, f32[2,256,1024]{2,1,0:T(8,128)S(1)}) fusion(f32[256,1024]{1,0:T(8,128)} %get-tuple-element.1392, f32[2]{0:T(128)} %get-tuple-element.1393, f32[256,1024]{1,0:T(8,128)S(1)} %get-tuple-element.1394, f32[2]{0:T(128)} %get-tuple-element.1395, f32[2,256]{1,0:T(2,128)S(1)} %fusion.372, ...), kind=kLoop, calls=%fused_computation.507.clone.1 | loop fusion | flops 72351232 | bytes 142873120 | tf_op jit(solution)/shard_map/while/body/eval_jaxpr/reduce_sum | solution.py:119
  2453.1 44.5 %multiply_multiply_fusion.4 = f32[2,261,1034]{2,1,0:T(8,128)} fusion(f32[2,256,1024]{2,1,0:T(8,128)S(1)} %copy-done.2, f32[261,1034]{1,0:T(8,128)} %fusion.373, f32[2]{0:T(128)S(1)} %get-tuple-element.1396, f32[2]{0:T(128)S(1)} %get-tuple-element.1397, f32[2]{0:T(128)S(1)} %get-tuple-element.1398, f32[2]{0:T(128)S(1)} %get-tuple-element.1399, ...), kind=kLoop, calls=%fused_computation.436.clone.1 | loop fusion | flops 71786448 | bytes 5336168 | tf_op jit(solution)/shard_map/while/body/eval_jaxpr/mul | solution.py:121
  2545.8 52.9 %collective-permute-done.13 = bf16[256,3072]{0,1:T(8,128)(2,1)} collective-permute-done((bf16[256,3072]{0,1:T(8,128)(2,1)}, bf16[256,3072]{0,1:T(8,128)(2,1)}, u32[]{:S(2)}, u32[]{:S(2)}) %collective-permute-start.13) | collective-permute-done | bytes 1572896 | tf_op jit(solution)/shard_map/ppermute | solution.py:14
  2637.7 157.0 %reduce-scatter.9.cloned.1.call-done = bf16[192,4608]{1,0:T(8,128)(2,1)} async-done(((bf16[1536,4608]{1,0:T(8,128)(2,1)}), bf16[192,4608]{1,0:T(8,128)(2,1)}) %reduce-scatter.9.cloned.1.call-update) | async-done | bytes 1769488 | tf_op jit(solution)/shard_map/reduce_scatter | solution.py:352
  2806.6 40.1 %all-reduce.2 = (f32[16,6,11]{2,0,1:T(8,128)S(1)}, f32[8,2,2]{0,2,1:T(2,128)}, f32[1536]{0:T(1024)}, f32[1536]{0:T(1024)}, f32[1536]{0:T(1024)}) all-reduce(f32[16,6,11]{2,0,1:T(8,128)S(1)} %bitcast.778, f32[8,2,2]{0,2,1:T(2,128)S(1)} %copy.255, f32[1536]{0:T(1024)S(1)} %get-tuple-element.619, ...), channel_id=1, replica_groups=mesh['rep'=4,'seq'=8] {'rep','seq'}, use_global_device_ids=true, to_apply=%region_89.90 | all-reduce | flops 5696 | bytes 45568 | tf_op jit(solution)/shard_map/psum | solution.py:360
  2850.3 102.6 %all-reduce.6.cloned.1.call-done = (bf16[192,4608]{1,0:T(8,128)(2,1)}, bf16[192,1536]{1,0:T(8,128)(2,1)}, bf16[1536,512]{1,0:T(8,128)(2,1)}, bf16[1536,512]{1,0:T(8,128)(2,1)}, bf16[512,1536]{1,0:T(8,128)(2,1)}) async-done(((bf16[192,4608]{1,0:T(8,128)(2,1)}, bf16[192,1536]{1,0:T(8,128)(2,1)}, bf16[1536,512]{1,0:T(8,128)(2,1)}, bf16[1536,512]{1,0:T(8,128)(2,1)}, bf16[512,1536]{1,0:T(8,128)(2,1)}), ...) | async-done | bytes 7077904 | tf_op jit(solution)/shard_map/psum | solution.py:364
  (2757 shorter events, 1653.2 us)
Async XLA Ops:
  7.2 808.8 %copy-start = (bf16[1536,512]{1,0:T(8,128)(2,1)S(1)}, bf16[1536,512]{1,0:T(8,128)(2,1)}, u32[]{:S(2)}) copy-start(bf16[1536,512]{1,0:T(8,128)(2,1)} %param.28) | copy-start | bytes 4718596
  7.2 134.8 %all-gather.4.cloned.1.call-start = ((), (), s32[]{:S(2)}) async-start(), calls=%async_computation.4 | async-start | bytes 15925248 | tf_op jit(solution)/shard_map/all_gather | solution.py:222
  8.0 645.8 %all-gather.6.cloned.1.call-start = ((), (), s32[]{:S(2)}) async-start(), calls=%async_computation.5 | async-start | bytes 5308416 | tf_op jit(solution)/shard_map/all_gather | solution.py:223
  8.7 781.0 %all-gather.8.cloned.1.call-start = ((), (), s32[]{:S(2)}) async-start(), calls=%async_computation.7 | async-start | bytes 7077888 | tf_op jit(solution)/shard_map/all_gather | solution.py:279
  154.1 67.7 %collective-permute-start = (bf16[256,3072]{1,0:T(8,128)(2,1)}, bf16[256,3072]{1,0:T(8,128)(2,1)}, u32[]{:S(2)}, u32[]{:S(2)}) collective-permute-start(bf16[256,3072]{1,0:T(8,128)(2,1)} %slice.2477), channel_id=1, source_target_pairs={{0,3},{1,4},{2,5},{3,6},{4,7},{8,11},{9,12},{10,13},{11,14},{12,15... | collective-permute-start | bytes 4718600 | tf_op jit(solution)/shard_map/ppermute | solution.py:14
  156.7 119.3 %collective-permute-start.1 = (bf16[256,3072]{1,0:T(8,128)(2,1)}, bf16[256,3072]{1,0:T(8,128)(2,1)}, u32[]{:S(2)}, u32[]{:S(2)}) collective-permute-start(bf16[256,3072]{1,0:T(8,128)(2,1)} %slice.2477), channel_id=1, source_target_pairs={{0,2},{1,3},{2,4},{3,5},{4,6},{5,7},{8,10},{9,11},{10,12},{11,13},... | collective-permute-start | bytes 4718600 | tf_op jit(solution)/shard_map/ppermute | solution.py:14
  161.4 114.6 %collective-permute-start.2 = (bf16[256,3072]{1,0:T(8,128)(2,1)}, bf16[256,3072]{1,0:T(8,128)(2,1)}, u32[]{:S(2)}, u32[]{:S(2)}) collective-permute-start(bf16[256,3072]{1,0:T(8,128)(2,1)} %slice.2477), channel_id=1, source_target_pairs={{0,1},{1,2},{2,3},{3,4},{4,5},{5,6},{6,7},{8,9},{9,10},{10,11},{11... | collective-permute-start | bytes 4718600 | tf_op jit(solution)/shard_map/ppermute | solution.py:14
  165.1 758.2 %reduce-scatter.7.cloned.1.call-start = ((), (), s32[]{:S(2)}) async-start(), calls=%async_computation.8 | async-start | bytes 7077888 | tf_op jit(solution)/shard_map/reduce_scatter | solution.py:293
  166.7 4.2 collective-permute-start.3
  659.5 54.0 %collective-permute-start.4 = (bf16[256,1536]{1,0:T(8,128)(2,1)S(1)}, bf16[256,1536]{1,0:T(8,128)(2,1)S(1)}, u32[]{:S(2)}, u32[]{:S(2)}) collective-permute-start(bf16[256,1536]{1,0:T(8,128)(2,1)S(1)} %multiply_convert_fusion.5), channel_id=1, source_target_pairs={{0,1},{1,2},{2,3},{3,4},{4,5},{5,6},{6,7},{7,0},{8,9},{9,10},{10,1... | collective-permute-start | bytes 2359304 | tf_op jit(solution)/shard_map/ppermute | solution.py:172
  713.5 14.1 collective-permute-start.5
  728.5 15.3 collective-permute-start.6
  744.6 13.5 collective-permute-start.7
  759.0 13.3 collective-permute-start.8
  772.4 13.5 collective-permute-start.9
  785.9 13.5 collective-permute-start.10
  839.8 153.8 %reduce-scatter.5.cloned.1.call-start = ((), (), s32[]{:S(2)}) async-start(), calls=%async_computation.6 | async-start | bytes 7077888 | tf_op jit(solution)/shard_map/reduce_scatter | solution.py:272
  848.1 1789.7 %reduce-scatter.11.cloned.1.call-start = ((), (), s32[]{:S(2)}) async-start(), calls=%async_computation.10 | async-start | bytes 5308416 | tf_op jit(solution)/shard_map/reduce_scatter | solution.py:355
  1023.1 1771.7 %reduce-scatter.9.cloned.1.call-start = ((), (), s32[]{:S(2)}) async-start(), calls=%async_computation.9 | async-start | bytes 15925248 | tf_op jit(solution)/shard_map/reduce_scatter | solution.py:352
  2532.5 13.3 collective-permute-start.12
  2533.8 64.9 %collective-permute-start.13 = (bf16[256,3072]{0,1:T(8,128)(2,1)}, bf16[256,3072]{0,1:T(8,128)(2,1)}, u32[]{:S(2)}, u32[]{:S(2)}) collective-permute-start(bf16[256,3072]{0,1:T(8,128)(2,1)} %get-tuple-element.859), channel_id=1, source_target_pairs={{2,0},{3,1},{4,2},{5,3},{6,4},{7,5},{10,8},{11,9},{12,10},{13,11},... | collective-permute-start | bytes 4718600 | tf_op jit(solution)/shard_map/ppermute | solution.py:14
  2535.1 68.8 %collective-permute-start.14 = (bf16[256,3072]{0,1:T(8,128)(2,1)}, bf16[256,3072]{0,1:T(8,128)(2,1)}, u32[]{:S(2)}, u32[]{:S(2)}) collective-permute-start(bf16[256,3072]{0,1:T(8,128)(2,1)} %get-tuple-element.858), channel_id=1, source_target_pairs={{3,0},{4,1},{5,2},{6,3},{7,4},{11,8},{12,9},{13,10},{14,11},{15,12... | collective-permute-start | bytes 4718600 | tf_op jit(solution)/shard_map/ppermute | solution.py:14
  2541.1 3.8 collective-permute-start.11
  2617.0 335.9 %all-reduce.6.cloned.1.call-start = ((), (), s32[]{:S(2)}) async-start(), calls=%async_computation.11 | async-start | bytes 14155776 | tf_op jit(solution)/shard_map/psum | solution.py:364
  (788 other events, 6419.6 us)
Sparse Core Ops, SparseCore 0:
  9.7 132.3 all-gather.3
  143.7 75.9 all-gather.5
  221.9 99.1 all-gather.7
  839.9 83.2 reduce-scatter.6
  925.4 68.1 reduce-scatter.4
  1023.2 53.3 reduce-scatter.10
  2617.2 177.5 reduce-scatter.8
  2800.2 152.6 all-reduce.5
